TPU v7x, 512 devices: a whole 4x8x8 slice. The times are simulated.
512 devices in a mesh: dp: 16 (over z, core), expert: 32 (over x, y).
Axes of the slice: x: 4, y: 8, z: 8, core: 2. Of those that a mesh axis runs over, the one named last changes fastest.
Arguments:
- layer_input: bfloat16 [1280, 4096], P('expert', 'dp'), may hold values from -6 to 6
- output_grad: bfloat16 [1280, 4096], P('expert', 'dp'), may hold values from -3 to 3
- route_ids: int32 [1280, 8], P('expert'), may hold values from 0 to 31, all different within a row; in each aligned block of 40 rows (0 to 39, 40 to 79, ...) at most 15 rows name the same one
- route_probs: bfloat16 [1280, 8], P('expert'), may hold values from 0.049804688 to 0.3984375
- gate_weight: bfloat16 [32, 4096, 1024], P('expert', 'dp'), may hold values from -0.09375 to 0.09375
- up_weight: bfloat16 [32, 4096, 1024], P('expert', 'dp'), may hold values from -0.09375 to 0.09375
- down_weight: bfloat16 [32, 1024, 4096], P('expert', None, 'dp'), may hold values from -0.1875 to 0.1875
Outputs:
- input_grad: bfloat16 [1280, 4096], P('expert', 'dp')
- prob_grad: bfloat16 [1280, 8], P('expert')
- gate_grad: bfloat16 [32, 4096, 1024], P('expert', 'dp')
- up_grad: bfloat16 [32, 4096, 1024], P('expert', 'dp')
- down_grad: bfloat16 [32, 1024, 4096], P('expert', None, 'dp')
Inputs may be any that keep to these rules, and one draw needn't show every extreme that they name: `route_ids`: each token names 8 different experts. In each aligned block of 40 tokens (the tokens of one index of the expert axis) at most 15 tokens name the same expert, and in every draw some expert is named by exactly 15 tokens of some block.
All inputs are finite; a program needn't handle non-finite values.
Results may differ from a plain program's by a relative error of at most 0.035.
Values may be sent and summed in bfloat16 or wider, within the bound.
A program may use at most 64 MiB of HBM per device.

v0:
```python
import jax
import jax.numpy as jnp
from jax import lax
from jax.sharding import PartitionSpec as P


def swiglu_back(gate_pre, up_pre, hidden_grad):
    sig_gate = jax.nn.sigmoid(gate_pre)
    active = (gate_pre * sig_gate * up_pre).astype(jnp.bfloat16)
    gate_delta = (hidden_grad * up_pre * sig_gate * (1.0 + gate_pre * (1.0 - sig_gate))).astype(
        jnp.bfloat16
    )
    up_delta = (hidden_grad * gate_pre * sig_gate).astype(jnp.bfloat16)
    return (active, gate_delta, up_delta)


def contract_last(left, right):
    return lax.dot_general(
        left, right, (((1,), (1,)), ((), ())), preferred_element_type=jnp.float32
    )


def on_device(
    layer_input, output_grad, route_ids, route_probs, gate_weight, up_weight, down_weight
):
    tok_count = layer_input.shape[0]
    width_part = layer_input.shape[1]
    chosen = route_ids.shape[1]
    experts = lax.axis_size("expert")
    capacity = 3 * tok_count * chosen // (2 * experts)
    row_count = experts * capacity
    cslots = jnp.arange(capacity, dtype=jnp.int32)
    expert_ids = jnp.arange(experts, dtype=jnp.int32)
    onehot = (route_ids[:, :, None] == expert_ids).astype(jnp.int32)
    member = jnp.sum(onehot, axis=1)
    before = jnp.cumsum(member, axis=0) - member
    pweight = jnp.sum(
        onehot.astype(jnp.float32) * route_probs.astype(jnp.float32)[:, :, None], axis=1
    )
    select = ((before[:, :, None] == cslots) & (member[:, :, None] > 0)).astype(jnp.bfloat16)
    send_x = jnp.einsum(
        "tec,td->ecd", select, layer_input, preferred_element_type=jnp.float32
    ).astype(jnp.bfloat16)
    send_g = jnp.einsum(
        "tec,td->ecd", select, output_grad, preferred_element_type=jnp.float32
    ).astype(jnp.bfloat16)
    send_p = jnp.einsum("tec,te->ec", select.astype(jnp.float32), pweight).astype(jnp.bfloat16)
    recv_x, recv_g, recv_p = (
        lax.all_to_all(send_x, "expert", split_axis=0, concat_axis=0, tiled=True),
        lax.all_to_all(send_g, "expert", split_axis=0, concat_axis=0, tiled=True),
        lax.all_to_all(send_p, "expert", split_axis=0, concat_axis=0, tiled=True),
    )
    rows_x = recv_x.reshape(row_count, width_part)
    rows_g = recv_g.reshape(row_count, width_part)
    rows_p = recv_p.reshape(row_count)
    gate_w = gate_weight[0]
    up_w = up_weight[0]
    down_w = down_weight[0]
    scaled = (rows_p.astype(jnp.float32)[:, None] * rows_g.astype(jnp.float32)).astype(jnp.bfloat16)
    gate_part = jnp.dot(rows_x, gate_w, preferred_element_type=jnp.float32)
    up_part = jnp.dot(rows_x, up_w, preferred_element_type=jnp.float32)
    grad_part = contract_last(scaled, down_w)
    gate_pre, up_pre, hidden_grad = (
        lax.psum(gate_part.astype(jnp.bfloat16), "dp").astype(jnp.float32),
        lax.psum(up_part.astype(jnp.bfloat16), "dp").astype(jnp.float32),
        lax.psum(grad_part.astype(jnp.bfloat16), "dp").astype(jnp.float32),
    )
    active, gate_delta, up_delta = swiglu_back(gate_pre, up_pre, hidden_grad)
    out_rows = jnp.dot(active, down_w, preferred_element_type=jnp.float32)
    dot_part = jnp.sum(rows_g.astype(jnp.float32) * out_rows, axis=1)
    gate_dot = lax.psum(dot_part, "dp").astype(jnp.bfloat16)
    down_grad = jnp.einsum("rf,rd->fd", active, scaled, preferred_element_type=jnp.float32).astype(
        jnp.bfloat16
    )[None]
    gate_grad = jnp.einsum(
        "rd,rf->df", rows_x, gate_delta, preferred_element_type=jnp.float32
    ).astype(jnp.bfloat16)[None]
    up_grad = jnp.einsum("rd,rf->df", rows_x, up_delta, preferred_element_type=jnp.float32).astype(
        jnp.bfloat16
    )[None]
    row_grad = (contract_last(gate_delta, gate_w) + contract_last(up_delta, up_w)).astype(
        jnp.bfloat16
    )
    back_x, back_p = (
        lax.all_to_all(
            row_grad.reshape(experts, capacity, width_part),
            "expert",
            split_axis=0,
            concat_axis=0,
            tiled=True,
        ),
        lax.all_to_all(
            gate_dot.reshape(experts, capacity), "expert", split_axis=0, concat_axis=0, tiled=True
        ),
    )
    input_sum = jnp.einsum("tec,ecd->td", select, back_x, preferred_element_type=jnp.float32)
    gate_table = jnp.einsum("tec,ec->te", select.astype(jnp.float32), back_p.astype(jnp.float32))
    input_grad = input_sum.astype(jnp.bfloat16)
    prob_grad = jnp.sum(onehot.astype(jnp.float32) * gate_table[:, None, :], axis=2).astype(
        jnp.bfloat16
    )
    return (input_grad, prob_grad, gate_grad, up_grad, down_grad)


def solution(mesh):
    placed = (
        P("expert", "dp"),
        P("expert", "dp"),
        P("expert", None),
        P("expert", None),
        P("expert", "dp", None),
        P("expert", "dp", None),
        P("expert", None, "dp"),
    )
    return jax.shard_map(
        on_device,
        mesh=mesh,
        in_specs=placed,
        out_specs=(
            P("expert", "dp"),
            P("expert", None),
            P("expert", "dp", None),
            P("expert", "dp", None),
            P("expert", None, "dp"),
        ),
        check_vma=False,
    )
```

profile of v0, /device:TPU:8, one launch (start us, length us, event | category | flops | bytes accessed | tf_op | source)
XLA Modules:
  0.0 364.9 jit_solution(10696455717776967576)
XLA Ops:
  7.2 0.8 convert_reduce_fusion
  8.2 0.9 convolution_convert_fusion.6
  9.3 22.2 %all_to_all.37 = bf16[32,15,256]{2,1,0:T(8,128)(2,1)S(1)} all-to-all(bf16[32,15,256]{2,1,0:T(8,128)(2,1)S(1)} %copy.51), channel_id=1, replica_groups=mesh['dp'=16,'expert'=32] {'expert'}, dimensions={0} | all-to-all | bytes 491520 | tf_op jit(solution)/shard_map/all_to_all | solution.py:49
  31.7 1.4 convolution_convert_fusion
  33.0 1.4 convolution_convert_fusion.1
  35.5 15.8 %all_to_all.38 = bf16[32,15,256]{2,1,0:T(8,128)(2,1)S(1)} all-to-all(bf16[32,15,256]{2,1,0:T(8,128)(2,1)S(1)} %copy.50), channel_id=1, replica_groups=mesh['dp'=16,'expert'=32] {'expert'}, dimensions={0} | all-to-all | bytes 491520 | tf_op jit(solution)/shard_map/all_to_all | solution.py:50
  51.4 103.7 %all-reduce.6.cloned.1.call-done = (bf16[480,1024]{1,0:T(8,128)(2,1)}, bf16[480,1024]{1,0:T(8,128)(2,1)}) async-done(((bf16[480,1024]{1,0:T(8,128)(2,1)}, bf16[480,1024]{1,0:T(8,128)(2,1)}), (bf16[480,1024]{1,0:T(8,128)(2,1)}, bf16[480,1024]{1,0:T(8,128)(2,1)})) %all-reduce.6.cloned.1.call-update) | async-done | bytes 1966096 | tf_op jit(solution)/shard_map/psum | solution.py:65
  155.2 2.2 fusion.3
  157.4 0.9 copy-done.1
  158.8 26.2 %psum.31 = bf16[480]{0:T(512)(128)(2,1)S(1)} all-reduce(f32[480]{0:T(512)S(1)} %fusion.14), channel_id=1, replica_groups=mesh['dp'=16,'expert'=32] {'dp'}, use_global_device_ids=true, to_apply=%region_7.8 | all-reduce | flops 480 | bytes 2880 | tf_op jit(solution)/shard_map/psum | solution.py:71
  185.1 0.7 all_to_all.31
  185.8 9.9 %all-to-all-start.4 = ((bf16[32,1,15]{2,1,0:T(2,128)(2,1)}), bf16[32,1,15]{2,1,0:T(2,128)(2,1)S(1)}, u32[]{:S(2)}, u32[]{:S(2)}) async-start(bf16[32,1,15]{2,1,0:T(2,128)(2,1)} %all_to_all.31), calls=%async_computation.4 | async-start | bytes 32768 | tf_op jit(solution)/shard_map/all_to_all | solution.py:92
  195.8 8.4 %all-to-all-done.4 = bf16[32,1,15]{2,1,0:T(2,128)(2,1)S(1)} async-done(((bf16[32,1,15]{2,1,0:T(2,128)(2,1)}), bf16[32,1,15]{2,1,0:T(2,128)(2,1)S(1)}, u32[]{:S(2)}, u32[]{:S(2)}) %all-to-all-start.4) | async-done | bytes 992 | tf_op jit(solution)/shard_map/all_to_all | solution.py:92
  205.7 12.8 %all_to_all.39 = bf16[32,1,15]{2,1,0:T(2,128)(2,1)S(1)} all-to-all(bf16[32,1,15]{2,1,0:T(2,128)(2,1)S(1)} %copy.49), channel_id=1, replica_groups=mesh['dp'=16,'expert'=32] {'expert'}, dimensions={0} | all-to-all | bytes 1920 | tf_op jit(solution)/shard_map/all_to_all | solution.py:51
  218.7 1.4 convolution_convert_fusion.2
  220.3 110.3 %all-reduce.4.cloned.1.call-done = bf16[480,1024]{1,0:T(8,128)(2,1)} async-done(((bf16[480,1024]{1,0:T(8,128)(2,1)}), bf16[480,1024]{1,0:T(8,128)(2,1)}) %all-reduce.4.cloned.1.call-update) | async-done | bytes 983056 | tf_op jit(solution)/shard_map/psum | solution.py:66
  330.6 2.8 fusion.9
  334.4 0.8 reshape.60
  335.2 9.9 %all-to-all-start.3 = ((bf16[32,15,256]{2,1,0:T(8,128)(2,1)}), bf16[32,15,256]{2,1,0:T(8,128)(2,1)}, u32[]{:S(2)}, u32[]{:S(2)}) async-start(bf16[32,15,256]{2,1,0:T(8,128)(2,1)} %reshape.60), calls=%async_computation.3 | async-start | bytes 524288 | tf_op jit(solution)/shard_map/all_to_all | solution.py:85
  345.1 2.6 fusion.12
  347.7 1.3 fusion.10
  348.9 1.3 fusion.11
  350.2 6.1 %all-to-all-done.3 = bf16[32,15,256]{2,1,0:T(8,128)(2,1)} async-done(((bf16[32,15,256]{2,1,0:T(8,128)(2,1)}), bf16[32,15,256]{2,1,0:T(8,128)(2,1)}, u32[]{:S(2)}, u32[]{:S(2)}) %all-to-all-start.3) | async-done | bytes 245792 | tf_op jit(solution)/shard_map/all_to_all | solution.py:85
  356.3 1.8 fusion.15
  (49 shorter events, 5.0 us)
Async XLA Ops:
  7.2 24.5 %copy-start = (bf16[1,256,1024]{2,1,0:T(8,128)(2,1)S(1)}, bf16[1,256,1024]{2,1,0:T(8,128)(2,1)}, u32[]{:S(2)}) copy-start(bf16[1,256,1024]{2,1,0:T(8,128)(2,1)} %param.11) | copy-start | bytes 1572868
  7.2 148.0 %all-reduce.6.cloned.1.call-start = ((), (), s32[]{:S(2)}) async-start(), calls=%async_computation.6 | async-start | bytes 3932160 | tf_op jit(solution)/shard_map/psum | solution.py:65
  31.7 1.4 copy-start.3
  34.4 0.7 copy-start.6
  51.4 105.9 %copy-start.4 = (f32[480,256]{1,0:T(8,128)}, f32[480,256]{1,0:T(8,128)S(1)}, u32[]{:S(2)}) copy-start(f32[480,256]{1,0:T(8,128)S(1)} %reshape.62) | copy-start | bytes 1474564
  155.2 3.2 copy-start.2
  157.4 1.0 copy-start.1
  158.3 37.4 %copy-start.8 = (bf16[40,8]{0,1:T(8,128)(2,1)S(1)}, bf16[40,8]{0,1:T(8,128)(2,1)}, u32[]{:S(2)}) copy-start(bf16[40,8]{0,1:T(8,128)(2,1)} %param.10) | copy-start | bytes 1924
  158.3 46.3 %copy-start.7 = (s32[40,8]{0,1:T(8,128)S(1)}, s32[40,8]{0,1:T(8,128)}, u32[]{:S(2)}) copy-start(s32[40,8]{0,1:T(8,128)} %param.9) | copy-start | bytes 3844
  185.8 18.4 %all-to-all-start.4 = ((bf16[32,1,15]{2,1,0:T(2,128)(2,1)}), bf16[32,1,15]{2,1,0:T(2,128)(2,1)S(1)}, u32[]{:S(2)}, u32[]{:S(2)}) async-start(bf16[32,1,15]{2,1,0:T(2,128)(2,1)} %all_to_all.31), calls=%async_computation.4 | async-start | bytes 32768 | tf_op jit(solution)/shard_map/all_to_all | solution.py:92
  195.7 135.0 %all-reduce.4.cloned.1.call-start = ((), (), s32[]{:S(2)}) async-start(), calls=%async_computation.5 | async-start | bytes 1966080 | tf_op jit(solution)/shard_map/psum | solution.py:66
  334.4 10.7 %copy-start.5 = (f32[480,256]{1,0:T(8,128)S(1)}, f32[480,256]{1,0:T(8,128)}, u32[]{:S(2)}) copy-start(f32[480,256]{1,0:T(8,128)} %copy-done.4) | copy-start | bytes 1474564
  335.2 21.1 %all-to-all-start.3 = ((bf16[32,15,256]{2,1,0:T(8,128)(2,1)}), bf16[32,15,256]{2,1,0:T(8,128)(2,1)}, u32[]{:S(2)}, u32[]{:S(2)}) async-start(bf16[32,15,256]{2,1,0:T(8,128)(2,1)} %reshape.60), calls=%async_computation.3 | async-start | bytes 524288 | tf_op jit(solution)/shard_map/all_to_all | solution.py:85
Sparse Core Ops, SparseCore 0:
  34.6 120.5 all-reduce.5
  220.3 110.3 all-reduce.3
where the time goes:
time: 366 us; the launch traced here: 365 us
  waiting for transfers between devices  229 us (63%)
  blocking collectives  77.1 us (21%)
  starting transfers between devices  19.8 us (5%)
  between operations  14.3 us (4%)
  matrix products  14 us (4%)
  other arithmetic  6.74 us (2%)
  local copies, waits for them, and re-layouts  4.39 us (1%)
    psum x1, waiting for transfers between devices, on_device(): lax.psum(grad_part.astype(jnp.bfloat16), 'dp').astype(jnp.float32)  110 us
    psum x1, waiting for transfers between devices, on_device(): lax.psum(up_part.astype(jnp.bfloat16), 'dp').astype(jnp.float32)  104 us
    psum x1, blocking collectives, on_device(): gate_dot = lax.psum(dot_part, 'dp').astype(jnp.bfloat16)  26.2 us
    all_to_all x1, blocking collectives, on_device(): lax.all_to_all(send_x, 'expert', split_axis=0, concat_axis=0, tiled=True)  22.2 us
    all_to_all x1, blocking collectives, on_device(): lax.all_to_all(send_g, 'expert', split_axis=0, concat_axis=0, tiled=True)  15.8 us
    all_to_all x1, blocking collectives, on_device(): lax.all_to_all(send_p, 'expert', split_axis=0, concat_axis=0, tiled=True)  12.8 us
    all_to_all x1, starting transfers between devices, on_device(): lax.all_to_all(row_grad.reshape(experts, capacity, width_part), 'expert',...  9.9 us
    all_to_all x1, starting transfers between devices, on_device(): lax.all_to_all(gate_dot.reshape(experts, capacity), 'expert', split_axis=...  9.85 us
  transfers between devices with their start and end apart: 4, of which 4 were waited for; matrix products, arithmetic and copies ran while one was open for 2% of the time, Pallas kernels for 0%

commit v1 on v0

--- a/solution.py
+++ b/solution.py
@@ -60,10 +60,16 @@
     gate_part = jnp.dot(rows_x, gate_w, preferred_element_type=jnp.float32)
     up_part = jnp.dot(rows_x, up_w, preferred_element_type=jnp.float32)
     grad_part = contract_last(scaled, down_w)
+
+    def load_levels_all_in(q_in):
+        mid_arr = lax.all_gather(q_in, "dp")
+        z1 = jnp.sum(mid_arr, axis=0)
+        return z1
+
     gate_pre, up_pre, hidden_grad = (
         lax.psum(gate_part.astype(jnp.bfloat16), "dp").astype(jnp.float32),
         lax.psum(up_part.astype(jnp.bfloat16), "dp").astype(jnp.float32),
-        lax.psum(grad_part.astype(jnp.bfloat16), "dp").astype(jnp.float32),
+        load_levels_all_in(grad_part.astype(jnp.bfloat16)).astype(jnp.float32),
     )
     active, gate_delta, up_delta = swiglu_back(gate_pre, up_pre, hidden_grad)
     out_rows = jnp.dot(active, down_w, preferred_element_type=jnp.float32)

time: 366 us -> 351 us (0.959)
  waiting for transfers between devices: 229 us -> 206 us
  other arithmetic: 6.74 us -> 16.5 us
    psum x1 -> x0, waiting for transfers between devices: 110 us -> none  [on_device(): lax.psum(grad_part.astype(jnp.bfloat16), 'dp').astype(jnp.float32)]
    all_gather x0 -> x1, waiting for transfers between devices: none -> 86.1 us  [load_levels_all_in(): mid_arr = lax.all_gather(q_in, 'dp')]
    reduce_sum x0 -> x1, other arithmetic: none -> 9.72 us  [load_levels_all_in(): z1 = jnp.sum(mid_arr, axis=0)]
where the time goes in v1:
time: 351 us
  waiting for transfers between devices  206 us (59%)
  blocking collectives  77.1 us (22%)
  starting transfers between devices  19.8 us (6%)
  other arithmetic  16.5 us (5%)
  between operations  14.3 us (4%)
  matrix products  13.2 us (4%)
  local copies, waits for them, and re-layouts  3.68 us (1%)
    psum x1, waiting for transfers between devices, on_device(): lax.psum(up_part.astype(jnp.bfloat16), 'dp').astype(jnp.float32)  104 us
    all_gather x1, waiting for transfers between devices, load_levels_all_in(): mid_arr = lax.all_gather(q_in, 'dp')  86.1 us
    psum x1, blocking collectives, on_device(): gate_dot = lax.psum(dot_part, 'dp').astype(jnp.bfloat16)  26.2 us
    all_to_all x1, blocking collectives, on_device(): lax.all_to_all(send_x, 'expert', split_axis=0, concat_axis=0, tiled=True)  22.2 us
    all_to_all x1, blocking collectives, on_device(): lax.all_to_all(send_g, 'expert', split_axis=0, concat_axis=0, tiled=True)  15.8 us
    all_to_all x1, blocking collectives, on_device(): lax.all_to_all(send_p, 'expert', split_axis=0, concat_axis=0, tiled=True)  12.8 us
    all_to_all x1, starting transfers between devices, on_device(): lax.all_to_all(gate_dot.reshape(experts, capacity), 'expert', split_axis=...  9.85 us
    all_to_all x1, starting transfers between devices, on_device(): lax.all_to_all(row_grad.reshape(experts, capacity, width_part), 'expert',...  9.84 us
  transfers between devices with their start and end apart: 4, of which 4 were waited for; matrix products, arithmetic and copies ran while one was open for 2% of the time, Pallas kernels for 0%

profile of v1, /device:TPU:8, one launch (start us, length us, event | category | flops | bytes accessed | tf_op | source)
XLA Modules:
  0.0 350.9 jit_solution(5003342842120151398)
XLA Ops:
  7.2 0.8 convert_reduce_fusion
  8.3 0.9 convolution_convert_fusion.6
  9.4 22.2 %all_to_all.37 = bf16[32,15,256]{2,1,0:T(8,128)(2,1)S(1)} all-to-all(bf16[32,15,256]{2,1,0:T(8,128)(2,1)S(1)} %copy.51), channel_id=1, replica_groups=mesh['dp'=16,'expert'=32] {'expert'}, dimensions={0} | all-to-all | bytes 491520 | tf_op jit(solution)/shard_map/all_to_all | solution.py:49
  31.7 1.4 convolution_convert_fusion
  33.1 1.4 convolution_convert_fusion.1
  34.9 15.8 %all_to_all.38 = bf16[32,15,256]{2,1,0:T(8,128)(2,1)S(1)} all-to-all(bf16[32,15,256]{2,1,0:T(8,128)(2,1)S(1)} %copy.50), channel_id=1, replica_groups=mesh['dp'=16,'expert'=32] {'expert'}, dimensions={0} | all-to-all | bytes 491520 | tf_op jit(solution)/shard_map/all_to_all | solution.py:50
  50.8 104.4 %all-reduce.3.cloned.1.call-done = (bf16[480,1024]{1,0:T(8,128)(2,1)}, bf16[480,1024]{1,0:T(8,128)(2,1)}) async-done(((bf16[480,1024]{1,0:T(8,128)(2,1)}, bf16[480,1024]{1,0:T(8,128)(2,1)}), (bf16[480,1024]{1,0:T(8,128)(2,1)}, bf16[480,1024]{1,0:T(8,128)(2,1)})) %all-reduce.3.cloned.1.call-update) | async-done | bytes 1966096 | tf_op jit(solution)/shard_map/psum | solution.py:71
  155.2 2.1 fusion.3
  157.4 1.0 copy-done.1
  158.9 26.2 %psum.23 = bf16[480]{0:T(512)(128)(2,1)S(1)} all-reduce(f32[480]{0:T(512)S(1)} %fusion.14), channel_id=1, replica_groups=mesh['dp'=16,'expert'=32] {'dp'}, use_global_device_ids=true, to_apply=%region_7.8 | all-reduce | flops 480 | bytes 2880 | tf_op jit(solution)/shard_map/psum | solution.py:77
  185.9 9.8 %all-to-all-start.4 = ((bf16[32,1,15]{2,1,0:T(2,128)(2,1)}), bf16[32,1,15]{2,1,0:T(2,128)(2,1)S(1)}, u32[]{:S(2)}, u32[]{:S(2)}) async-start(bf16[32,1,15]{2,1,0:T(2,128)(2,1)} %all_to_all.31), calls=%async_computation.4 | async-start | bytes 32768 | tf_op jit(solution)/shard_map/all_to_all | solution.py:98
  195.8 8.4 %all-to-all-done.4 = bf16[32,1,15]{2,1,0:T(2,128)(2,1)S(1)} async-done(((bf16[32,1,15]{2,1,0:T(2,128)(2,1)}), bf16[32,1,15]{2,1,0:T(2,128)(2,1)S(1)}, u32[]{:S(2)}, u32[]{:S(2)}) %all-to-all-start.4) | async-done | bytes 992 | tf_op jit(solution)/shard_map/all_to_all | solution.py:98
  205.7 12.8 %all_to_all.39 = bf16[32,1,15]{2,1,0:T(2,128)(2,1)S(1)} all-to-all(bf16[32,1,15]{2,1,0:T(2,128)(2,1)S(1)} %copy.49), channel_id=1, replica_groups=mesh['dp'=16,'expert'=32] {'expert'}, dimensions={0} | all-to-all | bytes 1920 | tf_op jit(solution)/shard_map/all_to_all | solution.py:51
  218.8 1.4 convolution_convert_fusion.2
  220.4 86.1 %all-gather.3.cloned.1.call-done = bf16[7680,1024]{1,0:T(8,128)(2,1)} async-done(((bf16[480,1024]{1,0:T(8,128)(2,1)}), bf16[7680,1024]{1,0:T(8,128)(2,1)}) %all-gather.3.cloned.1.call-update) | async-done | bytes 15728656 | tf_op jit(solution)/shard_map/all_gather | solution.py:65
  306.4 9.7 %reduce_sum.50 = bf16[480,1024]{1,0:T(8,128)(2,1)} reduce(bf16[16,480,1024]{2,1,0:T(8,128)(2,1)} %bitcast.61, bf16[]{:T(256)} %constant.10.clone.1), dimensions={0}, to_apply=%region_3.4 | reduce | flops 7372800 | bytes 16711682 | tf_op jit(solution)/shard_map/reduce_sum | solution.py:66
  316.2 2.8 fusion.9
  319.9 0.8 reshape.60
  320.7 9.8 %all-to-all-start.3 = ((bf16[32,15,256]{2,1,0:T(8,128)(2,1)}), bf16[32,15,256]{2,1,0:T(8,128)(2,1)S(1)}, u32[]{:S(2)}, u32[]{:S(2)}) async-start(bf16[32,15,256]{2,1,0:T(8,128)(2,1)} %reshape.60), calls=%async_computation.3 | async-start | bytes 524288 | tf_op jit(solution)/shard_map/all_to_all | solution.py:91
  330.6 2.7 fusion.12
  333.3 1.3 fusion.10
  334.5 1.3 fusion.11
  335.8 7.5 %all-to-all-done.3 = bf16[32,15,256]{2,1,0:T(8,128)(2,1)S(1)} async-done(((bf16[32,15,256]{2,1,0:T(8,128)(2,1)}), bf16[32,15,256]{2,1,0:T(8,128)(2,1)S(1)}, u32[]{:S(2)}, u32[]{:S(2)}) %all-to-all-start.3) | async-done | bytes 245792 | tf_op jit(solution)/shard_map/all_to_all | solution.py:91
  343.3 0.8 fusion.15
  (48 shorter events, 5.0 us)
Async XLA Ops:
  7.2 24.5 %copy-start = (bf16[1,256,1024]{2,1,0:T(8,128)(2,1)S(1)}, bf16[1,256,1024]{2,1,0:T(8,128)(2,1)}, u32[]{:S(2)}) copy-start(bf16[1,256,1024]{2,1,0:T(8,128)(2,1)} %param.11) | copy-start | bytes 1572868
  7.2 25.9 %copy-start.3 = (bf16[1,256,1024]{2,1,0:T(8,128)(2,1)S(1)}, bf16[1,256,1024]{2,1,0:T(8,128)(2,1)}, u32[]{:S(2)}) copy-start(bf16[1,256,1024]{2,1,0:T(8,128)(2,1)} %param.12) | copy-start | bytes 1572868
  7.2 148.0 %all-reduce.3.cloned.1.call-start = ((), (), s32[]{:S(2)}) async-start(), calls=%async_computation.6 | async-start | bytes 3932160 | tf_op jit(solution)/shard_map/psum | solution.py:71
  33.1 1.4 copy-start.5
  50.7 107.6 %copy-start.2 = (bf16[1,1024,256]{2,1,0:T(8,128)(2,1)S(1)}, bf16[1,1024,256]{2,1,0:T(8,128)(2,1)}, u32[]{:S(2)}) copy-start(bf16[1,1024,256]{2,1,0:T(8,128)(2,1)} %param.13) | copy-start | bytes 1572868
  50.8 108.1 %copy-start.4 = (f32[480,256]{1,0:T(8,128)}, f32[480,256]{1,0:T(8,128)S(1)}, u32[]{:S(2)}) copy-start(f32[480,256]{1,0:T(8,128)S(1)} %reshape.62) | copy-start | bytes 1474564
  155.2 40.6 %copy-start.7 = (bf16[40,8]{0,1:T(8,128)(2,1)S(1)}, bf16[40,8]{0,1:T(8,128)(2,1)}, u32[]{:S(2)}) copy-start(bf16[40,8]{0,1:T(8,128)(2,1)} %param.10) | copy-start | bytes 1924
  155.2 49.4 %copy-start.6 = (s32[40,8]{0,1:T(8,128)S(1)}, s32[40,8]{0,1:T(8,128)}, u32[]{:S(2)}) copy-start(s32[40,8]{0,1:T(8,128)} %param.9) | copy-start | bytes 3844
  157.4 1.0 copy-start.1
  185.9 18.4 %all-to-all-start.4 = ((bf16[32,1,15]{2,1,0:T(2,128)(2,1)}), bf16[32,1,15]{2,1,0:T(2,128)(2,1)S(1)}, u32[]{:S(2)}, u32[]{:S(2)}) async-start(bf16[32,1,15]{2,1,0:T(2,128)(2,1)} %all_to_all.31), calls=%async_computation.4 | async-start | bytes 32768 | tf_op jit(solution)/shard_map/all_to_all | solution.py:98
  195.7 110.7 %all-gather.3.cloned.1.call-start = ((), (), s32[]{:S(2)}) async-start(), calls=%async_computation.5 | async-start | bytes 16711680 | tf_op jit(solution)/shard_map/all_gather | solution.py:65
  320.7 22.5 %all-to-all-start.3 = ((bf16[32,15,256]{2,1,0:T(8,128)(2,1)}), bf16[32,15,256]{2,1,0:T(8,128)(2,1)S(1)}, u32[]{:S(2)}, u32[]{:S(2)}) async-start(bf16[32,15,256]{2,1,0:T(8,128)(2,1)} %reshape.60), calls=%async_computation.3 | async-start | bytes 524288 | tf_op jit(solution)/shard_map/all_to_all | solution.py:91
Sparse Core Ops, SparseCore 0:
  34.6 120.5 all-reduce.2
  220.3 86.0 all-gather.2
